TPU v7x, 256 devices: a whole 4x4x8 slice. The times are simulated.
256 devices in a mesh: sub: 2 (over core), row: 16 (over x, y), col: 8 (over z).
Axes of the slice: x: 4, y: 4, z: 8, core: 2. Of those that a mesh axis runs over, the one named last changes fastest.
Arguments:
- front: float32 [16384, 16384], P(('sub', 'row'), 'col'), as said below
- child_blocks: float32 [2, 8192, 8192], P('sub', 'row', 'col'), may hold values from -1 to 1
- child_map: int32 [2, 8192], replicated, may hold values from 0 to 16383, as said below
Outputs:
- factored: float32 [16384, 16384], P(('sub', 'row'), 'col')
Inputs may be any that keep to these rules, and one draw needn't show every extreme that they name: Each row of child_map is strictly increasing. Call block b the parent indices b * 32 to b * 32 + 31. Of the entries at positions k * 1024 to (k + 1) * 1024 - 1 of a row, exactly 128 lie in blocks whose number modulo 8 is d, for every k and d. Of the entries at positions k * 512 to (k + 1) * 512 - 1, at most 24 lie in blocks whose number modulo 32 is p, for every k and p; for each child some p takes exactly 24 from every k. The front's diagonal dominates the rows of the pivot block by construction.
All inputs are finite; a program needn't handle non-finite values.
Results may differ from a plain program's by a relative error of at most 0.00012.
Values sent between devices are 32-bit elements; how exact they have to be, the bound alone decides.
A program may use at most 128 MiB of HBM per device.

v0:
```python
import jax
import jax.numpy as jnp
from jax import lax
from jax.sharding import PartitionSpec as P

PW = 512
NB = 32


def from_root(value, axis, source):
    kept = jnp.where(lax.axis_index(axis) == source, value, 0).astype(value.dtype)
    return lax.psum(kept, axis)


def natural_index(local, group, groups):
    return (local // NB * groups + group) * NB + local % NB


def local_index(natural, groups):
    return natural // NB // groups * NB + natural % NB


def slot_ranks(owner, groups):
    member = (owner[:, None] == jnp.arange(groups, dtype=jnp.int32)[None, :]).astype(jnp.int32)
    return jnp.sum(jnp.cumsum(member, axis=0) * member, axis=1) - 1


def body(front, child_blocks, child_map):
    n_sub = lax.axis_size("sub")
    n_row = lax.axis_size("row")
    n_col = lax.axis_size("col")
    row_groups = n_sub * n_row
    row_group = lax.axis_index("sub") * n_row + lax.axis_index("row")
    col_group = lax.axis_index("col")
    local_rows, local_cols = front.shape
    natural_rows = natural_index(jnp.arange(local_rows, dtype=jnp.int32), row_group, row_groups)
    natural_cols = natural_index(jnp.arange(local_cols, dtype=jnp.int32), col_group, n_col)
    lower = natural_rows[:, None] >= natural_cols[None, :]
    assembled = jnp.where(lower, front, jnp.float32(0.0))
    contribution = child_blocks[0]
    child_rows, child_cols = contribution.shape
    own_map = lax.dynamic_index_in_dim(child_map, lax.axis_index("sub"), 0, keepdims=False)
    row_start = lax.axis_index("row") * child_rows
    col_start = col_group * child_cols
    child_row_ids = row_start + jnp.arange(child_rows, dtype=jnp.int32)
    child_col_ids = col_start + jnp.arange(child_cols, dtype=jnp.int32)
    contribution = jnp.where(
        child_row_ids[:, None] >= child_col_ids[None, :], contribution, jnp.float32(0.0)
    )
    row_targets = lax.dynamic_slice_in_dim(own_map, row_start, child_rows)
    col_targets = lax.dynamic_slice_in_dim(own_map, col_start, child_cols)
    per_dest = child_cols // n_col
    col_owner = col_targets // NB % n_col
    col_slots = col_owner * per_dest + slot_ranks(col_owner, n_col)
    col_order = (
        jnp.zeros((child_cols,), jnp.int32)
        .at[col_slots]
        .set(jnp.arange(child_cols, dtype=jnp.int32))
    )
    spans = 2 * child_rows // NB // row_groups
    capacity = NB // 2 * spans + NB // 4 * max(0, 2 - spans)
    buffer_rows = row_groups * capacity
    row_owner = row_targets // NB % row_groups
    row_slots = row_owner * capacity + slot_ranks(row_owner, row_groups)
    source_rows = (
        jnp.full((buffer_rows,), child_rows, jnp.int32)
        .at[row_slots]
        .set(jnp.arange(child_rows, dtype=jnp.int32))
    )
    filled = source_rows < child_rows
    source_rows = jnp.minimum(source_rows, child_rows - 1)
    by_column = contribution[:, col_order]
    moved = lax.all_to_all(by_column, "col", split_axis=1, concat_axis=1, tiled=True)
    packed = jnp.where(filled[:, None], moved[source_rows], jnp.float32(0.0))
    received = lax.all_to_all(packed, ("sub", "row"), split_axis=0, concat_axis=0, tiled=True)
    slots_child = n_row * capacity
    received_cols = received.shape[1]
    received = received.reshape(n_sub, slots_child, received_cols)
    for child in range(n_sub):
        full_map = child_map[child]
        col_mask = full_map // NB % n_col == col_group
        taken = jnp.nonzero(col_mask, size=received_cols)[0]
        col_index = local_index(full_map[taken], n_col)
        match = (
            (full_map // NB % row_groups == row_group).astype(jnp.int32).reshape(n_row, child_rows)
        )
        ranks = jnp.cumsum(match, axis=1) - 1
        slots = jnp.arange(n_row, dtype=jnp.int32)[:, None] * capacity + ranks
        slots = jnp.where(match > 0, slots, slots_child).reshape(-1)
        row_index = (
            jnp.full((slots_child,), local_rows, jnp.int32)
            .at[slots]
            .set(local_index(full_map, row_groups), mode="drop")
        )
        slot_of_row = (
            jnp.full((local_rows,), slots_child, jnp.int32)
            .at[row_index]
            .set(jnp.arange(slots_child, dtype=jnp.int32), mode="drop")
        )
        col_source = (
            jnp.full((local_cols,), received_cols, jnp.int32)
            .at[col_index]
            .set(jnp.arange(received_cols, dtype=jnp.int32), mode="drop")
        )
        row_inside = slot_of_row < slots_child
        col_inside = col_source < received_cols
        placed = received[child][jnp.minimum(slot_of_row, slots_child - 1)][
            :, jnp.minimum(col_source, received_cols - 1)
        ]
        assembled = assembled + jnp.where(
            row_inside[:, None] & col_inside[None, :], placed, jnp.float32(0.0)
        )
    panel_local = PW // n_col
    gathered = lax.all_gather(assembled[:, :panel_local], "col", axis=1, tiled=True)
    panel = (
        gathered.reshape(local_rows, n_col, panel_local // NB, NB)
        .transpose(0, 2, 1, 3)
        .reshape(local_rows, PW)
    )
    head_blocks = max(1, PW // (row_groups * NB))
    heading = lax.all_gather(panel[: head_blocks * NB], ("sub", "row"), axis=0, tiled=True)
    corner = (
        heading.reshape(row_groups, head_blocks, NB, PW).transpose(1, 0, 2, 3).reshape(-1, PW)[:PW]
    )
    pivot = jnp.tril(corner) + jnp.tril(corner, -1).T
    factor = jnp.linalg.cholesky(pivot)
    solved = lax.linalg.triangular_solve(
        factor, panel, left_side=False, lower=True, transpose_a=True
    )
    factor_rows = jnp.where(
        natural_rows[:, None] < PW, factor[jnp.clip(natural_rows, 0, PW - 1)], solved
    )
    spread = row_groups // n_col
    pieces = [
        from_root(factor_rows, ("sub", "row"), col_group + step * n_col) for step in range(spread)
    ]
    stacked = jnp.stack([piece.reshape(local_rows // NB, NB, PW) for piece in pieces], axis=1)
    factor_cols = stacked.reshape(local_cols, PW)
    product = lax.dot_general(
        factor_rows,
        factor_cols,
        (((1,), (1,)), ((), ())),
        precision=lax.Precision.HIGHEST,
        preferred_element_type=jnp.float32,
    )
    update = assembled - product
    update = update.at[:, :panel_local].set(factor_rows[:, natural_cols[:panel_local]])
    return jnp.where(lower, update, jnp.float32(0.0))


def solution(mesh):
    return jax.shard_map(
        body,
        mesh=mesh,
        in_specs=(P(("sub", "row"), "col"), P("sub", "row", "col"), P()),
        out_specs=P(("sub", "row"), "col"),
        check_vma=False,
    )
```

profile of v0, /device:TPU:6, one launch (start us, length us, event | category | flops | bytes accessed | tf_op | source)
XLA Modules:
  0.0 718.6 jit_solution(14528451676120354646)
XLA Ops:
  7.3 2.3 reduce-window.74
  11.0 4.3 scatter_custom_fusion.5
  15.4 2.9 copy.57
  20.1 4.9 gather_fusion.1
  25.0 8.6 %all-to-all-start = ((f32[512,8,128]{0,2,1:T(8,128)}), f32[512,8,128]{0,2,1:T(8,128)S(1)}, u32[]{:S(2)}, u32[]{:S(2)}) async-start(f32[512,8,128]{0,2,1:T(8,128)} %bitcast.218), calls=%async_computation | async-start | bytes 4194304 | tf_op jit(solution)/shard_map/all_to_all | solution.py:73
  39.4 56.9 %scatter_custom_fusion.2 = s32[1024]{0:T(1024)S(1)} fusion(s32[8192]{0:T(1024)S(1)} %bitcast.238, s32[8192]{0:T(1024)S(1)} %ne.666, s32[]{:T(128)} %constant.510.clone.1), kind=kCustom, calls=%fused_computation.418 | custom fusion | flops 8192 | bytes 4100 | tf_op jit(solution)/shard_map/scatter-add | solution.py:82
  97.5 2.4 scatter_custom_fusion.4
  101.6 6.2 gather_fusion
  107.7 56.8 %scatter_custom_fusion.8 = s32[1024]{0:T(1024)S(1)} fusion(s32[8192]{0:T(1024)S(1)} %bitcast.237, s32[8192]{0:T(1024)S(1)} %ne.666, s32[]{:T(128)} %constant.510.clone.1), kind=kCustom, calls=%fused_computation.416 | custom fusion | flops 8192 | bytes 4100 | tf_op jit(solution)/shard_map/scatter-add | solution.py:82
  165.9 6.2 gather_fusion.5
  172.6 30.6 %scatter_custom_fusion = s32[384]{0:T(512)S(1)} fusion(s32[8192]{0:T(1024)S(1)} %bitcast.236, s32[8192]{0:T(1024)S(1)} %get-tuple-element.71, s32[]{:T(128)} %constant.522.clone.1), kind=kCustom, calls=%fused_computation.433 | custom fusion | bytes 1540 | tf_op jit(solution)/shard_map/scatter | solution.py:93
  206.6 3.6 gather_fusion.2
  210.2 3.8 broadcast_select_fusion
  214.0 7.6 %all-to-all-start.1 = ((f32[32,24,1024]{2,1,0:T(8,128)}), f32[32,24,1024]{2,1,0:T(8,128)}, u32[]{:S(2)}, u32[]{:S(2)}) async-start(f32[32,24,1024]{2,1,0:T(8,128)} %broadcast_select_fusion), calls=%async_computation.1 | async-start | bytes 6291456 | tf_op jit(solution)/shard_map/all_to_all | solution.py:75
  221.8 4.3 scatter_custom_fusion.3
  226.1 30.4 %scatter_custom_fusion.6 = s32[384]{0:T(512)S(1)} fusion(s32[8192]{0:T(1024)S(1)} %bitcast.235, s32[8192]{0:T(1024)S(1)} %get-tuple-element.68, s32[]{:T(128)} %constant.522.clone.1), kind=kCustom, calls=%fused_computation.431 | custom fusion | bytes 1540 | tf_op jit(solution)/shard_map/scatter | solution.py:93
  256.6 2.9 scatter_custom_fusion.1
  259.5 2.9 scatter_custom_fusion.7
  262.5 4.3 scatter_custom_fusion.9
  267.0 3.4 fusion.149
  270.4 2.6 gather_fusion.3
  274.9 8.9 %gather_fusion.4 = f32[2048,512]{1,0:T(8,128)} fusion(f32[512,1024]{0,1:T(8,128)S(1)} %copy.59, s32[2048]{0:T(1024)S(1)} %fusion.85), kind=kCustom, calls=%fused_computation.4 | custom fusion | bytes 8396800 | tf_op jit(solution)/shard_map/gather | solution.py:107
  283.8 5.5 copy.60
  289.3 2.6 gather_fusion.6
  293.9 8.9 %gather_fusion.7 = f32[2048,512]{1,0:T(8,128)} fusion(f32[512,1024]{0,1:T(8,128)S(1)} %copy.66, s32[2048]{0:T(1024)S(1)} %fusion.86), kind=kCustom, calls=%fused_computation.7 | custom fusion | bytes 8396800 | tf_op jit(solution)/shard_map/gather | solution.py:107
  302.8 5.4 copy.67
  308.2 5.6 fusion.1
  316.7 40.4 %all-gather.3.cloned.1.call-done = f32[512,512]{0,1:T(8,128)} async-done(((f32[512,64]{0,1:T(8,128)}), f32[512,512]{0,1:T(8,128)}) %all-gather.3.cloned.1.call-update) | async-done | bytes 1048592 | tf_op jit(solution)/shard_map/all_gather | solution.py:114
  362.9 43.7 %all-gather.5.cloned.1.call-done = f32[1024,512]{1,0:T(8,128)} async-done(((f32[32,512]{1,0:T(8,128)}), f32[1024,512]{1,0:T(8,128)}) %all-gather.5.cloned.1.call-update) | async-done | bytes 2097168 | tf_op jit(solution)/shard_map/all_gather | solution.py:121
  411.2 11.7 %cholesky.103 = f32[128,128]{1,0:T(8,128)S(1)} custom-call(f32[128,128]{1,0:T(8,128)S(1)} %cholesky.263), custom_call_target="Cholesky" | custom-call | tf_op jit(solution)/shard_map/jit(cholesky)/cholesky | solution.py:126
  423.1 9.8 %custom-call.30 = f32[1,128,128]{1,2,0:T(8,128)S(1)} custom-call(f32[1,128,128]{2,1,0:T(8,128)S(1)} %get-tuple-element.62), custom_call_target="InvertDiagBlocksLowerTriangular" | custom-call | tf_op jit(solution)/shard_map/jit(cholesky)/cholesky | solution.py:126
  435.5 11.7 %cholesky.215 = f32[128,128]{1,0:T(8,128)S(1)} custom-call(f32[128,128]{1,0:T(8,128)S(1)} %cholesky.267), custom_call_target="Cholesky" | custom-call | tf_op jit(solution)/shard_map/jit(cholesky)/cholesky | solution.py:126
  448.6 10.0 %custom-call.31 = f32[1,128,128]{1,2,0:T(8,128)S(1)} custom-call(f32[1,128,128]{2,1,0:T(8,128)S(1)} %get-tuple-element.59), custom_call_target="InvertDiagBlocksLowerTriangular" | custom-call | tf_op jit(solution)/shard_map/jit(cholesky)/cholesky | solution.py:126
  460.1 11.7 %cholesky.236 = f32[128,128]{1,0:T(8,128)S(1)} custom-call(f32[128,128]{1,0:T(8,128)S(1)} %cholesky.272), custom_call_target="Cholesky" | custom-call | tf_op jit(solution)/shard_map/jit(cholesky)/cholesky | solution.py:126
  472.6 9.8 %custom-call.32 = f32[1,128,128]{1,2,0:T(8,128)S(1)} custom-call(f32[1,128,128]{2,1,0:T(8,128)S(1)} %get-tuple-element.56), custom_call_target="InvertDiagBlocksLowerTriangular" | custom-call | tf_op jit(solution)/shard_map/jit(cholesky)/cholesky | solution.py:126
  483.8 11.9 %cholesky.253 = f32[128,128]{1,0:T(8,128)S(1)} custom-call(f32[128,128]{1,0:T(8,128)S(1)} %convolution_subtract_fusion.6), custom_call_target="Cholesky" | custom-call | tf_op jit(solution)/shard_map/jit(cholesky)/cholesky | solution.py:126
  500.3 14.1 %while.2 = (s32[]{:T(128)}, f32[512,512]{1,0:T(8,128)}, s32[4,2]{0,1:T(2,128)S(1)}, f32[4,128,128]{2,1,0:T(8,128)}, s32[]{:T(128)}) while((s32[]{:T(128)}, f32[512,512]{1,0:T(8,128)}, s32[4,2]{0,1:T(2,128)S(1)}, f32[4,128,128]{2,1,0:T(8,128)}, s32[]{:T(128)}) %tuple.45), condition=%wide.while_cond.1, body=%wide.while_body.1.sunk | while | flops 2 | bytes 132705 | solution.py:127
  501.0 2.9 bitcast_dynamic-update-slice_fusion.2
  504.5 2.9 bitcast_dynamic-update-slice_fusion.2
  508.0 2.9 bitcast_dynamic-update-slice_fusion.2
  511.6 2.8 bitcast_dynamic-update-slice_fusion.2
  514.4 40.1 %custom-call.33 = f32[4,128,128]{1,2,0:T(8,128)S(1)} custom-call(f32[4,128,128]{2,1,0:T(8,128)} %get-tuple-element.24), custom_call_target="InvertDiagBlocksLowerTriangular" | custom-call | tf_op jit(solution)/shard_map/triangular_solve | solution.py:127
  558.0 2.0 convolution_subtract_fusion.1
  561.5 2.4 convolution_subtract_fusion.3
  571.7 120.7 %all-reduce.4.cloned.1.call-done = (f32[16,1,32,512]{3,2,1,0:T(8,128)}, f32[16,1,32,512]{3,2,1,0:T(8,128)}, f32[16,1,32,512]{3,2,1,0:T(8,128)}, f32[16,1,32,512]{3,2,1,0:T(8,128)}) async-done(((f32[16,1,32,512]{3,2,1,0:T(8,128)}, f32[16,1,32,512]{3,2,1,0:T(8,128)}, f32[16,1,32,512]{3,2,1,0:T(8,128)}, f32[16,1,32,512]{3,2,1,0:T(8,128)}), (f32[16,1,32,512]{3,2,1,0:T(8,128)}, f32[16,1,32,512]{3,2,1,0:T(8,128)}, ...) | async-done | bytes 4194320 | tf_op jit(solution)/shard_map/psum | solution.py:12
  692.4 2.8 pad_maximum_fusion
  695.8 6.8 convolution_subtract_fusion
  707.1 4.6 compare_select_fusion
  (195 shorter events, 65.0 us)
Async XLA Ops:
  25.0 8.6 %copy-start.7 = (s32[2,8192]{1,0:T(2,128)S(1)}, s32[2,8192]{1,0:T(2,128)}, u32[]{:S(2)}) copy-start(s32[2,8192]{1,0:T(2,128)} %param.7) | copy-start | bytes 196612
  25.0 178.4 %all-to-all-start = ((f32[512,8,128]{0,2,1:T(8,128)}), f32[512,8,128]{0,2,1:T(8,128)S(1)}, u32[]{:S(2)}, u32[]{:S(2)}) async-start(f32[512,8,128]{0,2,1:T(8,128)} %bitcast.218), calls=%async_computation | async-start | bytes 4194304 | tf_op jit(solution)/shard_map/all_to_all | solution.py:73
  203.3 1.3 copy-start.4
  214.0 53.0 %all-to-all-start.1 = ((f32[32,24,1024]{2,1,0:T(8,128)}), f32[32,24,1024]{2,1,0:T(8,128)}, u32[]{:S(2)}, u32[]{:S(2)}) async-start(f32[32,24,1024]{2,1,0:T(8,128)} %broadcast_select_fusion), calls=%async_computation.1 | async-start | bytes 6291456 | tf_op jit(solution)/shard_map/all_to_all | solution.py:75
  221.6 135.5 %all-gather.3.cloned.1.call-start = ((), (), s32[]{:S(2)}) async-start(), calls=%async_computation.2 | async-start | bytes 1179648 | tf_op jit(solution)/shard_map/all_gather | solution.py:114
  283.8 5.5 copy-start
  313.8 2.0 copy-start.1
  316.6 90.0 %all-gather.5.cloned.1.call-start = ((), (), s32[]{:S(2)}) async-start(), calls=%async_computation.3 | async-start | bytes 2162688 | tf_op jit(solution)/shard_map/all_gather | solution.py:121
  359.1 333.3 %all-reduce.4.cloned.1.call-start = ((), (), s32[]{:S(2)}) async-start(), calls=%async_computation.4 | async-start | bytes 8388608 | tf_op jit(solution)/shard_map/psum | solution.py:12
  410.2 1.0 copy-start.5
  500.3 61.2 %copy-start.6 = (f32[512,128]{1,0:T(8,128)S(1)}, f32[512,128]{1,0:T(8,128)}, u32[]{:S(2)}) copy-start(f32[512,128]{1,0:T(8,128)} %copy.90) | copy-start | bytes 786436
  554.5 0.7 copy-start.8
  692.4 3.4 copy-start.2
  702.7 2.0 copy-start.3
Sparse Core Ops, SparseCore 0:
  316.7 40.3 all-gather.2
  359.7 46.8 all-gather.4
  569.8 122.5 all-reduce.3
where the time goes:
time: 728 us; the launch traced here: 719 us
  other arithmetic  273 us (38%)
  waiting for transfers between devices  205 us (28%)
  local copies, waits for them, and re-layouts  185 us (25%)
  matrix products  22.3 us (3%)
  between operations  17.1 us (2%)
  starting transfers between devices  16.8 us (2%)
    psum x1, waiting for transfers between devices, from_root(): return lax.psum(kept, axis)  121 us
    scatter-add x2, other arithmetic, body(): taken = jnp.nonzero(col_mask, size=received_cols)[0]  114 us
    another operation x15, other arithmetic, body(): factor = jnp.linalg.cholesky(pivot)  79.5 us
    scatter x2, local copies, waits for them, and re-layouts, body(): row_index = jnp.full((slots_child,), local_rows, jnp.int32).at[slots].set...  61.1 us
    all_gather x1, waiting for transfers between devices, body(): lax.all_gather(panel[:head_blocks * NB], ('sub', 'row'), axis=0, tiled=True)  43.7 us
    another operation x3, other arithmetic, body(): lax.linalg.triangular_solve(factor, panel, left_side=False, lower=True, t...  41.4 us
    all_gather x1, waiting for transfers between devices, body(): lax.all_gather(assembled[:, :panel_local], 'col', axis=1, tiled=True)  40.4 us
    gather x8, local copies, waits for them, and re-layouts, body(): received[child][jnp.minimum(slot_of_row, slots_child - 1)]  37.8 us
  transfers between devices with their start and end apart: 5, of which 3 were waited for; matrix products, arithmetic and copies ran while one was open for 31% of the time, Pallas kernels for 0%

commit v1 on v0

--- a/solution.py
+++ b/solution.py
@@ -5,6 +5,12 @@
 
 PW = 512
 NB = 32
+
+
+def in_order(tiles, dim):
+    shape = list(tiles.shape[1:])
+    shape[dim] *= tiles.shape[0]
+    return jnp.moveaxis(tiles, 0, dim).reshape(shape)
 
 
 def from_root(value, axis, source):
@@ -111,7 +117,20 @@
             row_inside[:, None] & col_inside[None, :], placed, jnp.float32(0.0)
         )
     panel_local = PW // n_col
-    gathered = lax.all_gather(assembled[:, :panel_local], "col", axis=1, tiled=True)
+    x = assembled[:, :panel_local]
+    size = lax.axis_size("col")
+    pairs = [(i, (i + 1) % size) for i in range(size)]
+    back = [(b, a) for a, b in pairs]
+    lower_2, upper = ([], [])
+    for k in range(size - 1):
+        if k % 2 == 0:
+            lower_2.append(lax.ppermute(lower_2[-1] if lower_2 else x, "col", pairs))
+        else:
+            upper.append(lax.ppermute(upper[-1] if upper else x, "col", back))
+    blocks = jnp.stack([*lower_2[::-1], x, *upper])
+    shift = lax.axis_index("col") - len(lower_2)
+    blocks = blocks[(jnp.arange(size) - shift) % size]
+    gathered = in_order(blocks, 1)
     panel = (
         gathered.reshape(local_rows, n_col, panel_local // NB, NB)
         .transpose(0, 2, 1, 3)

time: 728 us -> 723 us (level)
  waiting for transfers between devices: 205 us -> 191 us
  starting transfers between devices: 16.8 us -> 28.4 us
  matrix products: 22.3 us -> 14.7 us
    all_gather x1 -> x0, waiting for transfers between devices: 40.4 us -> none  [body(): lax.all_gather(assembled[:, :panel_local], 'col', axis=1, tiled=True)]
    ppermute x0 -> x7, waiting for transfers between devices: none -> 23.2 us  [the longest x4 23.2 us: body(): lower_2.append(lax.ppermute(lower_2[-1] if lower_2 else x, 'col', pairs))]
    ppermute x0 -> x7, starting transfers between devices: none -> 11.9 us  [the longest x3 9.53 us: body(): upper.append(lax.ppermute(upper[-1] if upper else x, 'col', back))]
    another operation x27 -> x28, local copies, waits for them, and re-layouts: 15.8 us -> 16.5 us
  transfers between devices with their start and end apart: 5 -> 11, of which waited for: 3 -> 6; matrix products, arithmetic and copies ran while one was open for 31% -> 31% of each run, Pallas kernels for 0% -> 0%
where the time goes in v1:
time: 723 us; the launch traced here: 715 us
  other arithmetic  273 us (38%)
  waiting for transfers between devices  191 us (26%)
  local copies, waits for them, and re-layouts  190 us (26%)
  starting transfers between devices  28.4 us (4%)
  between operations  17.2 us (2%)
  matrix products  14.7 us (2%)
    psum x1, waiting for transfers between devices, from_root(): return lax.psum(kept, axis)  121 us
    scatter-add x2, other arithmetic, body(): taken = jnp.nonzero(col_mask, size=received_cols)[0]  114 us
    another operation x15, other arithmetic, body(): factor = jnp.linalg.cholesky(pivot)  79.7 us
    scatter x2, local copies, waits for them, and re-layouts, body(): row_index = jnp.full((slots_child,), local_rows, jnp.int32).at[slots].set...  61.3 us
    all_gather x1, waiting for transfers between devices, body(): lax.all_gather(panel[:head_blocks * NB], ('sub', 'row'), axis=0, tiled=True)  47.5 us
    another operation x3, other arithmetic, body(): lax.linalg.triangular_solve(factor, panel, left_side=False, lower=True, t...  41.4 us
    gather x8, local copies, waits for them, and re-layouts, body(): received[child][jnp.minimum(slot_of_row, slots_child - 1)]  37.8 us
    ppermute x4, waiting for transfers between devices, body(): lower_2.append(lax.ppermute(lower_2[-1] if lower_2 else x, 'col', pairs))  23.2 us
  transfers between devices with their start and end apart: 11, of which 6 were waited for; matrix products, arithmetic and copies ran while one was open for 31% of the time, Pallas kernels for 0%

profile of v1, /device:TPU:6, one launch (start us, length us, event | category | flops | bytes accessed | tf_op | source)
XLA Modules:
  0.0 714.6 jit_solution(5475664692647860487)
XLA Ops:
  11.1 2.9 copy.25
  14.0 4.3 scatter_custom_fusion.5
  20.1 4.9 gather_fusion.1
  25.0 8.6 %all-to-all-start = ((f32[512,8,128]{0,2,1:T(8,128)}), f32[512,8,128]{0,2,1:T(8,128)S(1)}, u32[]{:S(2)}, u32[]{:S(2)}) async-start(f32[512,8,128]{0,2,1:T(8,128)} %bitcast.237), calls=%async_computation | async-start | bytes 4194304 | tf_op jit(solution)/shard_map/all_to_all | solution.py:79
  39.4 56.9 %scatter_custom_fusion.2 = s32[1024]{0:T(1024)S(1)} fusion(s32[8192]{0:T(1024)S(1)} %bitcast.260, s32[8192]{0:T(1024)S(1)} %ne.688, s32[]{:T(128)} %constant.522.clone.1), kind=kCustom, calls=%fused_computation.431 | custom fusion | flops 8192 | bytes 4100 | tf_op jit(solution)/shard_map/scatter-add | solution.py:88
  101.6 6.2 gather_fusion
  107.8 56.8 %scatter_custom_fusion.8 = s32[1024]{0:T(1024)S(1)} fusion(s32[8192]{0:T(1024)S(1)} %bitcast.259, s32[8192]{0:T(1024)S(1)} %ne.688, s32[]{:T(128)} %constant.522.clone.1), kind=kCustom, calls=%fused_computation.429 | custom fusion | flops 8192 | bytes 4100 | tf_op jit(solution)/shard_map/scatter-add | solution.py:88
  165.9 6.2 gather_fusion.5
  172.7 30.9 %scatter_custom_fusion = s32[384]{0:T(512)S(1)} fusion(s32[8192]{0:T(1024)S(1)} %bitcast.258, s32[8192]{0:T(1024)S(1)} %get-tuple-element.68, s32[]{:T(128)} %constant.534.clone.1), kind=kCustom, calls=%fused_computation.447 | custom fusion | bytes 1540 | tf_op jit(solution)/shard_map/scatter | solution.py:99
  206.8 3.6 gather_fusion.2
  210.5 3.8 broadcast_select_fusion
  214.3 7.6 %all-to-all-start.1 = ((f32[32,24,1024]{2,1,0:T(8,128)}), f32[32,24,1024]{2,1,0:T(8,128)}, u32[]{:S(2)}, u32[]{:S(2)}) async-start(f32[32,24,1024]{2,1,0:T(8,128)} %broadcast_select_fusion), calls=%async_computation.1 | async-start | bytes 6291456 | tf_op jit(solution)/shard_map/all_to_all | solution.py:81
  222.0 4.3 scatter_custom_fusion.3
  226.4 30.4 %scatter_custom_fusion.6 = s32[384]{0:T(512)S(1)} fusion(s32[8192]{0:T(1024)S(1)} %bitcast.257, s32[8192]{0:T(1024)S(1)} %get-tuple-element.65, s32[]{:T(128)} %constant.534.clone.1), kind=kCustom, calls=%fused_computation.445 | custom fusion | bytes 1540 | tf_op jit(solution)/shard_map/scatter | solution.py:99
  256.8 2.9 scatter_custom_fusion.1
  259.8 2.9 scatter_custom_fusion.7
  262.8 4.5 scatter_custom_fusion.9
  267.4 3.4 fusion.151
  275.4 8.9 %gather_fusion.4 = f32[2048,512]{1,0:T(8,128)} fusion(f32[512,1024]{0,1:T(8,128)S(1)} %copy.27, s32[2048]{0:T(1024)S(1)} %fusion.85), kind=kCustom, calls=%fused_computation.4 | custom fusion | bytes 8396800 | tf_op jit(solution)/shard_map/gather | solution.py:113
  284.3 5.5 copy.28
  294.3 8.9 %gather_fusion.7 = f32[2048,512]{1,0:T(8,128)} fusion(f32[512,1024]{0,1:T(8,128)S(1)} %copy.34, s32[2048]{0:T(1024)S(1)} %fusion.86), kind=kCustom, calls=%fused_computation.7 | custom fusion | bytes 8396800 | tf_op jit(solution)/shard_map/gather | solution.py:113
  303.2 5.4 copy.35
  308.6 5.6 fusion.1
  318.4 8.1 %collective-permute-done = f32[512,64]{1,0:T(8,128)S(1)} collective-permute-done((f32[512,64]{1,0:T(8,128)S(1)}, f32[512,64]{1,0:T(8,128)S(1)}, u32[]{:S(2)}, u32[]{:S(2)}) %collective-permute-start) | collective-permute-done | bytes 131104 | tf_op jit(solution)/shard_map/ppermute | solution.py:127
  326.8 3.0 collective-permute-start.4
  329.8 5.9 collective-permute-done.1
  335.7 3.2 collective-permute-start.5
  338.9 5.0 collective-permute-done.2
  343.9 3.3 collective-permute-start.6
  347.2 4.2 collective-permute-done.3
  363.5 47.5 %all-gather.2.cloned.1.call-done = f32[1024,512]{1,0:T(8,128)} async-done(((f32[32,512]{1,0:T(8,128)}), f32[1024,512]{1,0:T(8,128)}) %all-gather.2.cloned.1.call-update) | async-done | bytes 2097168 | tf_op jit(solution)/shard_map/all_gather | solution.py:140
  414.6 11.7 %cholesky.103 = f32[128,128]{1,0:T(8,128)S(1)} custom-call(f32[128,128]{1,0:T(8,128)S(1)} %cholesky.263), custom_call_target="Cholesky" | custom-call | tf_op jit(solution)/shard_map/jit(cholesky)/cholesky | solution.py:145
  426.5 9.8 %custom-call.30 = f32[1,128,128]{1,2,0:T(8,128)S(1)} custom-call(f32[1,128,128]{2,1,0:T(8,128)S(1)} %get-tuple-element.59), custom_call_target="InvertDiagBlocksLowerTriangular" | custom-call | tf_op jit(solution)/shard_map/jit(cholesky)/cholesky | solution.py:145
  437.0 11.7 %cholesky.215 = f32[128,128]{1,0:T(8,128)S(1)} custom-call(f32[128,128]{1,0:T(8,128)S(1)} %cholesky.267), custom_call_target="Cholesky" | custom-call | tf_op jit(solution)/shard_map/jit(cholesky)/cholesky | solution.py:145
  450.1 10.2 %custom-call.31 = f32[1,128,128]{1,2,0:T(8,128)S(1)} custom-call(f32[1,128,128]{2,1,0:T(8,128)S(1)} %get-tuple-element.56), custom_call_target="InvertDiagBlocksLowerTriangular" | custom-call | tf_op jit(solution)/shard_map/jit(cholesky)/cholesky | solution.py:145
  460.9 11.7 %cholesky.236 = f32[128,128]{1,0:T(8,128)S(1)} custom-call(f32[128,128]{1,0:T(8,128)S(1)} %cholesky.272), custom_call_target="Cholesky" | custom-call | tf_op jit(solution)/shard_map/jit(cholesky)/cholesky | solution.py:145
  473.4 9.8 %custom-call.32 = f32[1,128,128]{1,2,0:T(8,128)S(1)} custom-call(f32[1,128,128]{2,1,0:T(8,128)S(1)} %get-tuple-element.53), custom_call_target="InvertDiagBlocksLowerTriangular" | custom-call | tf_op jit(solution)/shard_map/jit(cholesky)/cholesky | solution.py:145
  483.8 11.9 %cholesky.253 = f32[128,128]{1,0:T(8,128)S(1)} custom-call(f32[128,128]{1,0:T(8,128)S(1)} %convolution_subtract_fusion.6), custom_call_target="Cholesky" | custom-call | tf_op jit(solution)/shard_map/jit(cholesky)/cholesky | solution.py:145
  500.3 14.1 %while.2 = (s32[]{:T(128)}, f32[512,512]{1,0:T(8,128)}, s32[4,2]{0,1:T(2,128)S(1)}, f32[4,128,128]{2,1,0:T(8,128)}, s32[]{:T(128)}) while((s32[]{:T(128)}, f32[512,512]{1,0:T(8,128)}, s32[4,2]{0,1:T(2,128)S(1)}, f32[4,128,128]{2,1,0:T(8,128)}, s32[]{:T(128)}) %tuple.44), condition=%wide.while_cond.1, body=%wide.while_body.1.sunk | while | flops 2 | bytes 132705 | solution.py:146
  500.9 2.9 bitcast_dynamic-update-slice_fusion.10
  504.5 2.9 bitcast_dynamic-update-slice_fusion.10
  508.0 2.9 bitcast_dynamic-update-slice_fusion.10
  511.5 2.8 bitcast_dynamic-update-slice_fusion.10
  514.3 40.1 %custom-call.33 = f32[4,128,128]{1,2,0:T(8,128)S(1)} custom-call(f32[4,128,128]{2,1,0:T(8,128)} %get-tuple-element.24), custom_call_target="InvertDiagBlocksLowerTriangular" | custom-call | tf_op jit(solution)/shard_map/triangular_solve | solution.py:146
  567.5 120.8 %all-reduce.4.cloned.1.call-done = (f32[16,1,32,512]{3,2,1,0:T(8,128)}, f32[16,1,32,512]{3,2,1,0:T(8,128)}, f32[16,1,32,512]{3,2,1,0:T(8,128)}, f32[16,1,32,512]{3,2,1,0:T(8,128)}) async-done(((f32[16,1,32,512]{3,2,1,0:T(8,128)}, f32[16,1,32,512]{3,2,1,0:T(8,128)}, f32[16,1,32,512]{3,2,1,0:T(8,128)}, f32[16,1,32,512]{3,2,1,0:T(8,128)}), (f32[16,1,32,512]{3,2,1,0:T(8,128)}, f32[16,1,32,512]{3,2,1,0:T(8,128)}, ...) | async-done | bytes 4194320 | tf_op jit(solution)/shard_map/psum | solution.py:18
  688.3 2.8 pad_maximum_fusion
  691.7 6.8 convolution_subtract_fusion
  703.0 4.6 compare_select_fusion
  (208 shorter events, 78.6 us)
Async XLA Ops:
  25.0 8.6 %copy-start.6 = (s32[2,8192]{1,0:T(2,128)S(1)}, s32[2,8192]{1,0:T(2,128)}, u32[]{:S(2)}) copy-start(s32[2,8192]{1,0:T(2,128)} %param.7) | copy-start | bytes 196612
  25.0 178.6 %all-to-all-start = ((f32[512,8,128]{0,2,1:T(8,128)}), f32[512,8,128]{0,2,1:T(8,128)S(1)}, u32[]{:S(2)}, u32[]{:S(2)}) async-start(f32[512,8,128]{0,2,1:T(8,128)} %bitcast.237), calls=%async_computation | async-start | bytes 4194304 | tf_op jit(solution)/shard_map/all_to_all | solution.py:79
  203.6 1.3 copy-start.4
  214.3 53.1 %all-to-all-start.1 = ((f32[32,24,1024]{2,1,0:T(8,128)}), f32[32,24,1024]{2,1,0:T(8,128)}, u32[]{:S(2)}, u32[]{:S(2)}) async-start(f32[32,24,1024]{2,1,0:T(8,128)} %broadcast_select_fusion), calls=%async_computation.1 | async-start | bytes 6291456 | tf_op jit(solution)/shard_map/all_to_all | solution.py:81
  221.9 189.0 %all-gather.2.cloned.1.call-start = ((), (), s32[]{:S(2)}) async-start(), calls=%async_computation.2 | async-start | bytes 2162688 | tf_op jit(solution)/shard_map/all_gather | solution.py:140
  284.3 5.5 copy-start
  314.2 2.0 copy-start.1
  316.3 10.3 %collective-permute-start = (f32[512,64]{1,0:T(8,128)S(1)}, f32[512,64]{1,0:T(8,128)S(1)}, u32[]{:S(2)}, u32[]{:S(2)}) collective-permute-start(f32[512,64]{1,0:T(8,128)S(1)} %slice.282), channel_id=1, source_target_pairs={{0,1},{1,2},{2,3},{3,4},{4,5},{5,6},{6,7},{7,0},{8,9},{9,10},{10,1... | collective-permute-start | bytes 393224 | tf_op jit(solution)/shard_map/ppermute | solution.py:127
  326.6 9.1 %collective-permute-start.1 = (f32[512,64]{1,0:T(8,128)S(1)}, f32[512,64]{1,0:T(8,128)S(1)}, u32[]{:S(2)}, u32[]{:S(2)}) collective-permute-start(f32[512,64]{1,0:T(8,128)S(1)} %collective-permute-done), channel_id=1, source_target_pairs={{0,1},{1,2},{2,3},{3,4},{4,5},{5,6},{6,7},{7,0},{8,9},{9,10},{10,1... | collective-permute-start | bytes 393224 | tf_op jit(solution)/shard_map/ppermute | solution.py:127
  326.8 8.9 %collective-permute-start.4 = (f32[512,64]{1,0:T(8,128)S(1)}, f32[512,64]{1,0:T(8,128)S(1)}, u32[]{:S(2)}, u32[]{:S(2)}) collective-permute-start(f32[512,64]{1,0:T(8,128)S(1)} %slice.282), channel_id=1, source_target_pairs={{1,0},{2,1},{3,2},{4,3},{5,4},{6,5},{7,6},{0,7},{9,8},{10,9},{11,1... | collective-permute-start | bytes 393224 | tf_op jit(solution)/shard_map/ppermute | solution.py:129
  335.7 8.2 %collective-permute-start.2 = (f32[512,64]{1,0:T(8,128)S(1)}, f32[512,64]{1,0:T(8,128)S(1)}, u32[]{:S(2)}, u32[]{:S(2)}) collective-permute-start(f32[512,64]{1,0:T(8,128)S(1)} %collective-permute-done.1), channel_id=1, source_target_pairs={{0,1},{1,2},{2,3},{3,4},{4,5},{5,6},{6,7},{7,0},{8,9},{9,10},{10,1... | collective-permute-start | bytes 393224 | tf_op jit(solution)/shard_map/ppermute | solution.py:127
  335.7 8.2 %collective-permute-start.5 = (f32[512,64]{1,0:T(8,128)S(1)}, f32[512,64]{1,0:T(8,128)S(1)}, u32[]{:S(2)}, u32[]{:S(2)}) collective-permute-start(f32[512,64]{1,0:T(8,128)S(1)} %collective-permute-done.4), channel_id=1, source_target_pairs={{1,0},{2,1},{3,2},{4,3},{5,4},{6,5},{7,6},{0,7},{9,8},{10,9},{11,1... | collective-permute-start | bytes 393224 | tf_op jit(solution)/shard_map/ppermute | solution.py:129
  343.9 7.6 %collective-permute-start.3 = (f32[512,64]{1,0:T(8,128)S(1)}, f32[512,64]{1,0:T(8,128)S(1)}, u32[]{:S(2)}, u32[]{:S(2)}) collective-permute-start(f32[512,64]{1,0:T(8,128)S(1)} %collective-permute-done.2), channel_id=1, source_target_pairs={{0,1},{1,2},{2,3},{3,4},{4,5},{5,6},{6,7},{7,0},{8,9},{9,10},{10,1... | collective-permute-start | bytes 393224 | tf_op jit(solution)/shard_map/ppermute | solution.py:127
  343.9 13.6 %collective-permute-start.6 = (f32[512,64]{1,0:T(8,128)S(1)}, f32[512,64]{1,0:T(8,128)S(1)}, u32[]{:S(2)}, u32[]{:S(2)}) collective-permute-start(f32[512,64]{1,0:T(8,128)S(1)} %collective-permute-done.5), channel_id=1, source_target_pairs={{1,0},{2,1},{3,2},{4,3},{5,4},{6,5},{7,6},{0,7},{9,8},{10,9},{11,1... | collective-permute-start | bytes 393224 | tf_op jit(solution)/shard_map/ppermute | solution.py:129
  362.1 326.2 %all-reduce.4.cloned.1.call-start = ((), (), s32[]{:S(2)}) async-start(), calls=%async_computation.3 | async-start | bytes 8388608 | tf_op jit(solution)/shard_map/psum | solution.py:18
  483.8 70.7 %copy-start.5 = (f32[512,2,8,32]{0,3,2,1:T(8,128)S(1)}, f32[512,2,8,32]{0,3,2,1:T(8,128)}, u32[]{:S(2)}) copy-start(f32[512,2,8,32]{0,3,2,1:T(8,128)} %copy.40) | copy-start | bytes 3145732
  688.3 3.4 copy-start.2
  698.6 2.0 copy-start.3
Sparse Core Ops, SparseCore 0:
  362.2 48.7 all-gather.1
  565.6 122.5 all-reduce.3
